TPU v7x, 256 devices: a whole 4x4x8 slice. The times are simulated.
256 devices in a mesh: blk: 32 (over z, y_lo, core), head: 8 (over x, y_hi).
Axes of the slice: x: 4, y: 4 (y_hi: 2, y_lo: 2; y = y_hi * 2 + y_lo), z: 8, core: 2. Of those that a mesh axis runs over, the one named last changes fastest.
Arguments:
- query: bfloat16 [32768, 4096], P(('blk', 'head')), may hold values from -6 to 6
- key: bfloat16 [32768, 1024], P(('blk', 'head')), may hold values from -6 to 6
- value: bfloat16 [32768, 1024], P(('blk', 'head')), may hold values from -6 to 6
- grad_out: bfloat16 [32768, 4096], P(('blk', 'head')), may hold values from -6 to 6
- doc_lengths: int32 [64], replicated, may hold values from 1 to 1024, 32768 in all
Outputs:
- attended: bfloat16 [32768, 4096], P(('blk', 'head'))
- grad_query: bfloat16 [32768, 4096], P(('blk', 'head'))
- grad_key: bfloat16 [32768, 1024], P(('blk', 'head'))
- grad_value: bfloat16 [32768, 1024], P(('blk', 'head'))
Inputs may be any that keep to these rules, and one draw needn't show every extreme that they name: `doc_lengths`: every document has at most 1024 tokens, one has exactly 1024, and the lengths sum to 32768.
All inputs are finite; a program needn't handle non-finite values.
Results may differ from a plain program's by a relative error of at most 0.0088.
Values may be sent and summed in bfloat16 or wider, within the bound.
No kernel may reach another device: no remote copies, remote signals or barrier semaphores. Data moves between devices by JAX's collectives and lax.ppermute only.
A program may use at most 128 MiB of HBM per device.

v0:
```python
import jax
import jax.numpy as jnp
from jax import lax
from jax.sharding import PartitionSpec as P

HEAD_DIM = 128


def passed_along(value, axis, steps):
    count = lax.axis_size(axis)
    initial, last = (max(0, -steps), min(count, count - steps))
    return lax.ppermute(value, axis, [(source, source + steps) for source in range(initial, last)])


def segment_ids(positions, doc_starts):
    return jnp.sum((doc_starts[None, :] <= positions[:, None]).astype(jnp.int32), axis=1) - 1


def per_device(query, key, value, grad_out, doc_lengths):
    scaling = HEAD_DIM ** (-0.5)
    query_heads, key_heads, value_heads, grad_heads = (
        lax.all_to_all(query, "head", split_axis=1, concat_axis=0, tiled=True),
        lax.all_to_all(key, "head", split_axis=1, concat_axis=0, tiled=True),
        lax.all_to_all(value, "head", split_axis=1, concat_axis=0, tiled=True),
        lax.all_to_all(grad_out, "head", split_axis=1, concat_axis=0, tiled=True),
    )
    block_rows = query_heads.shape[0]
    pair_width = key_heads.shape[1]
    kv_local = pair_width // HEAD_DIM
    groups = query_heads.shape[1] // pair_width
    width_local = query_heads.shape[1]
    tile_rows = min(512, block_rows)
    tile_count = block_rows // tile_rows
    span_rows = block_rows + tile_rows
    block_index = lax.axis_index("blk")
    doc_ends = jnp.cumsum(doc_lengths)
    doc_starts = doc_ends - doc_lengths
    offsets = jnp.arange(tile_rows, dtype=jnp.int32)
    reaches = jnp.arange(span_rows, dtype=jnp.int32)
    paired = jnp.concatenate([key_heads, value_heads], axis=1)
    earlier = passed_along(paired, "blk", 1)
    window = jnp.concatenate([earlier, paired], axis=0)

    def tile_scores(tile_number):
        first_row = tile_number * tile_rows
        query_rows = lax.dynamic_slice_in_dim(query_heads, first_row, tile_rows, 0).reshape(
            tile_rows, kv_local, groups, HEAD_DIM
        )
        span_pairs = lax.dynamic_slice_in_dim(window, first_row, span_rows, 0)
        key_rows = span_pairs[:, :pair_width].reshape(span_rows, kv_local, HEAD_DIM)
        value_rows = span_pairs[:, pair_width:].reshape(span_rows, kv_local, HEAD_DIM)
        query_pos = block_index * block_rows + first_row + offsets
        key_pos = block_index * block_rows + first_row - block_rows + reaches
        allowed = (key_pos[None, :] <= query_pos[:, None]) & (
            segment_ids(query_pos, doc_starts)[:, None] == segment_ids(key_pos, doc_starts)[None, :]
        )
        scores = (
            jnp.einsum("qkgd,skd->kgqs", query_rows, key_rows, preferred_element_type=jnp.float32)
            * scaling
        )
        scores = jnp.where(allowed[None, None], scores, -jnp.inf)
        return (query_rows, key_rows, value_rows, scores)

    def forward_tile(tile_number):
        query_rows, key_rows, value_rows, scores = tile_scores(tile_number)
        peak_score = jnp.max(scores, axis=-1, keepdims=True)
        log_total = peak_score + jnp.log(
            jnp.sum(jnp.exp(scores - peak_score), axis=-1, keepdims=True)
        )
        weights_bf = jnp.exp(scores - log_total).astype(jnp.bfloat16)
        attended_rows = jnp.einsum(
            "kgqs,skd->qkgd", weights_bf, value_rows, preferred_element_type=jnp.float32
        )
        return (
            attended_rows.astype(jnp.bfloat16).reshape(tile_rows, width_local),
            log_total[..., 0],
        )

    tile_numbers = jnp.arange(tile_count, dtype=jnp.int32)
    attended_tiles, log_totals = lax.map(forward_tile, tile_numbers)
    attended_heads = attended_tiles.reshape(block_rows, width_local)

    def backward_tile(carry_sums, inputs):
        tile_number, log_total = inputs
        query_rows, key_rows, value_rows, scores = tile_scores(tile_number)
        first_row = tile_number * tile_rows
        grad_rows = lax.dynamic_slice_in_dim(grad_heads, first_row, tile_rows, 0).reshape(
            tile_rows, kv_local, groups, HEAD_DIM
        )
        output_rows = lax.dynamic_slice_in_dim(attended_heads, first_row, tile_rows, 0).reshape(
            tile_rows, kv_local, groups, HEAD_DIM
        )
        row_delta = jnp.einsum(
            "qkgd,qkgd->kgq", grad_rows, output_rows, preferred_element_type=jnp.float32
        )
        weights = jnp.exp(scores - log_total[..., None])
        weights_bf = weights.astype(jnp.bfloat16)
        value_part = jnp.einsum(
            "kgqs,qkgd->skd", weights_bf, grad_rows, preferred_element_type=jnp.float32
        )
        grad_weights = jnp.einsum(
            "qkgd,skd->kgqs", grad_rows, value_rows, preferred_element_type=jnp.float32
        )
        grad_scores = (weights * (grad_weights - row_delta[..., None])).astype(jnp.bfloat16)
        grad_query_rows = (
            jnp.einsum("kgqs,skd->qkgd", grad_scores, key_rows, preferred_element_type=jnp.float32)
            * scaling
        ).astype(jnp.bfloat16)
        key_part = (
            jnp.einsum(
                "kgqs,qkgd->skd", grad_scores, query_rows, preferred_element_type=jnp.float32
            )
            * scaling
        )
        partial_value = jnp.concatenate(
            [key_part.reshape(span_rows, pair_width), value_part.reshape(span_rows, pair_width)],
            axis=1,
        )
        current = lax.dynamic_slice_in_dim(carry_sums, first_row, span_rows, 0)
        carry_sums = lax.dynamic_update_slice_in_dim(
            carry_sums, current + partial_value, first_row, 0
        )
        return (carry_sums, grad_query_rows.reshape(tile_rows, width_local))

    start_sums = jnp.zeros((2 * block_rows, 2 * pair_width), jnp.float32)
    totals, grad_tiles = lax.scan(backward_tile, start_sums, (tile_numbers, log_totals))
    returned = passed_along(totals[:block_rows].astype(jnp.bfloat16), "blk", -1).astype(jnp.float32)
    own_sums = totals[block_rows:] + returned
    grad_key_heads = own_sums[:, :pair_width].astype(jnp.bfloat16)
    grad_value_heads = own_sums[:, pair_width:].astype(jnp.bfloat16)
    grad_query_heads = grad_tiles.reshape(block_rows, width_local)
    attended, grad_query, grad_key, grad_value = (
        lax.all_to_all(attended_heads, "head", split_axis=0, concat_axis=1, tiled=True),
        lax.all_to_all(grad_query_heads, "head", split_axis=0, concat_axis=1, tiled=True),
        lax.all_to_all(grad_key_heads, "head", split_axis=0, concat_axis=1, tiled=True),
        lax.all_to_all(grad_value_heads, "head", split_axis=0, concat_axis=1, tiled=True),
    )
    return (attended, grad_query, grad_key, grad_value)


def solution(mesh):
    in_specs = (
        P(("blk", "head"), None),
        P(("blk", "head"), None),
        P(("blk", "head"), None),
        P(("blk", "head"), None),
        P(),
    )
    out_specs = (
        P(("blk", "head"), None),
        P(("blk", "head"), None),
        P(("blk", "head"), None),
        P(("blk", "head"), None),
    )
    return jax.shard_map(
        per_device, mesh=mesh, in_specs=in_specs, out_specs=out_specs, check_vma=False
    )
```

profile of v0, /device:TPU:192, one launch (start us, length us, event | category | flops | bytes accessed | tf_op | source)
XLA Modules:
  0.0 260.8 jit_solution(13670175670676676605)
XLA Ops:
  2.3 6.9 %all-to-all-start = ((bf16[128,8,128]{2,0,1:T(8,128)(2,1)}), bf16[128,8,128]{2,0,1:T(8,128)(2,1)S(1)}, u32[]{:S(2)}, u32[]{:S(2)}) async-start(bf16[128,8,128]{2,0,1:T(8,128)(2,1)} %copy_bitcast_fusion.1), calls=%async_computation | async-start | bytes 524288 | tf_op jit(solution)/shard_map/all_to_all | solution.py:23
  9.3 1.7 copy_bitcast_fusion
  11.0 7.0 %all-to-all-done = bf16[128,8,128]{2,0,1:T(8,128)(2,1)S(1)} async-done(((bf16[128,8,128]{2,0,1:T(8,128)(2,1)}), bf16[128,8,128]{2,0,1:T(8,128)(2,1)S(1)}, u32[]{:S(2)}, u32[]{:S(2)}) %all-to-all-start) | async-done | bytes 262176 | tf_op jit(solution)/shard_map/all_to_all | solution.py:23
  18.0 3.4 %all-to-all-start.1 = ((bf16[128,8,128]{2,0,1:T(8,128)(2,1)}), bf16[128,8,128]{2,0,1:T(8,128)(2,1)S(1)}, u32[]{:S(2)}, u32[]{:S(2)}) async-start(bf16[128,8,128]{2,0,1:T(8,128)(2,1)} %copy_bitcast_fusion), calls=%async_computation.1 | async-start | bytes 524288 | tf_op jit(solution)/shard_map/all_to_all | solution.py:24
  21.4 2.3 copy.134
  23.7 6.1 %all-to-all-done.1 = bf16[128,8,128]{2,0,1:T(8,128)(2,1)S(1)} async-done(((bf16[128,8,128]{2,0,1:T(8,128)(2,1)}), bf16[128,8,128]{2,0,1:T(8,128)(2,1)S(1)}, u32[]{:S(2)}, u32[]{:S(2)}) %all-to-all-start.1) | async-done | bytes 262176 | tf_op jit(solution)/shard_map/all_to_all | solution.py:24
  29.8 3.6 %all-to-all-start.2 = ((bf16[128,8,512]{0,2,1:T(8,128)(2,1)}), bf16[128,8,512]{0,2,1:T(8,128)(2,1)S(1)}, u32[]{:S(2)}, u32[]{:S(2)}) async-start(bf16[128,8,512]{0,2,1:T(8,128)(2,1)} %bitcast.7), calls=%async_computation.2 | async-start | bytes 2097152 | tf_op jit(solution)/shard_map/all_to_all | solution.py:22
  33.4 1.9 collective-permute-start
  37.0 2.3 copy.139
  39.3 9.7 %collective-permute-done = bf16[1024,256]{1,0:T(8,128)(2,1)S(1)} collective-permute-done((bf16[1024,256]{1,0:T(8,128)(2,1)S(1)}, bf16[1024,256]{1,0:T(8,128)(2,1)S(1)}, u32[]{:S(2)}, u32[]{:S(2)}) %collective-permute-start) | collective-permute-done | bytes 524320 | tf_op jit(solution)/shard_map/ppermute | solution.py:12
  50.1 6.2 %all-to-all-start.4 = ((bf16[128,8,512]{0,2,1:T(8,128)(2,1)}), bf16[128,8,512]{0,2,1:T(8,128)(2,1)S(1)}, u32[]{:S(2)}, u32[]{:S(2)}) async-start(bf16[128,8,512]{0,2,1:T(8,128)(2,1)} %bitcast.14), calls=%async_computation.4 | async-start | bytes 2097152 | tf_op jit(solution)/shard_map/all_to_all | solution.py:25
  56.3 1.3 copy.135
  57.6 2.3 copy.136
  60.9 46.9 %while.32 = (s32[]{:T(128)}, bf16[2,512,512]{2,1,0:T(8,128)(2,1)}, f32[2,1,4,512]{3,2,1,0:T(4,128)S(1)}, s32[2]{0:T(128)S(1)}, bf16[2048,256]{1,0:T(8,128)(2,1)}...) while((s32[]{:T(128)}, bf16[2,512,512]{2,1,0:T(8,128)(2,1)}, ...), condition=%wide.region_6.7_spmd.clone, body=%wide.region_1.6_spmd.clone.sunk | while | flops 1648230400 | bytes 96331064 | solution.py:80
  64.6 3.1 %fusion.84 = (f32[4,512]{1,0:T(4,128)S(1)}, f32[1536,512,4]{1,0,2:T(8,128)S(1)}) fusion(pred[512,1536]{0,1:T(8,128)(4,1)S(1)} %compare_and_fusion.4, bf16[512,4,128]{0,2,1:T(8,128)(2,1)S(1)} %bitcast.238, bf16[2048,256]{1,0:T(8,128)(2,1)} %get-tuple-element.674, s32[]{:T(128)S(6)} %select_n.92), kind=kOutput, calls=%fused_computation.7.clone.1 | convolution fusion | flops 814741504 | bytes 14295044 | tf_op jit(solution)/shard_map/while/body/eval_jaxpr/qkgd,skd->kgqs/dot_general | solution.py:58
  67.8 4.6 %copy-done.2 = f32[1536,512,4]{1,0,2:T(8,128)} copy-done((f32[1536,512,4]{1,0,2:T(8,128)}, f32[1536,512,4]{1,0,2:T(8,128)S(1)}, u32[]{:S(2)}) %copy-start.2) | copy-done | bytes 12582936 | tf_op jit(solution)/shard_map/while
  72.4 2.7 %exponential_reduce_fusion.2 = f32[4,512]{1,0:T(4,128)S(1)} fusion(f32[1536,512,4]{1,0,2:T(8,128)S(1)} %get-tuple-element.623, f32[4,512]{1,0:T(4,128)S(1)} %get-tuple-element.624, pred[512,1536]{0,1:T(8,128)(4,1)S(1)} %compare_and_fusion.4), kind=kLoop, calls=%fused_computation.6.clone.1 | loop fusion | flops 12580864 | bytes 13385728 | tf_op jit(solution)/shard_map/while/body/eval_jaxpr/reduce_sum | solution.py:68
  75.1 8.2 %fusion.85 = bf16[128,4,512]{2,0,1:T(8,128)(2,1)S(1)} fusion(f32[1536,512,4]{1,0,2:T(8,128)} %copy-done.2, f32[4,512]{1,0:T(4,128)S(1)} %get-tuple-element.625, pred[512,1536]{0,1:T(8,128)(4,1)S(1)} %compare_and_fusion.4, bf16[2048,256]{1,0:T(8,128)(2,1)} %get-tuple-element.674, s32[]{:T(128)S(6)} %select_n.92, s32[]{:T(128)S(6)} %add.279), kind=kOutput, calls=%fused_computation.12.clone.1 | convolution fusion | flops 818151424 | bytes 14295048 | tf_op jit(solution)/shard_map/while/body/eval_jaxpr/kgqs,skd->qkgd/dot_general | solution.py:71
  88.1 3.2 %fusion.84 = (f32[4,512]{1,0:T(4,128)S(1)}, f32[1536,512,4]{1,0,2:T(8,128)S(1)}) fusion(pred[512,1536]{0,1:T(8,128)(4,1)S(1)} %compare_and_fusion.4, bf16[512,4,128]{0,2,1:T(8,128)(2,1)S(1)} %bitcast.238, bf16[2048,256]{1,0:T(8,128)(2,1)} %get-tuple-element.674, s32[]{:T(128)S(6)} %select_n.92), kind=kOutput, calls=%fused_computation.7.clone.1 | convolution fusion | flops 814741504 | bytes 14295044 | tf_op jit(solution)/shard_map/while/body/eval_jaxpr/qkgd,skd->kgqs/dot_general | solution.py:58
  91.3 4.6 %copy-done.2 = f32[1536,512,4]{1,0,2:T(8,128)} copy-done((f32[1536,512,4]{1,0,2:T(8,128)}, f32[1536,512,4]{1,0,2:T(8,128)S(1)}, u32[]{:S(2)}) %copy-start.2) | copy-done | bytes 12582936 | tf_op jit(solution)/shard_map/while
  95.8 2.7 %exponential_reduce_fusion.2 = f32[4,512]{1,0:T(4,128)S(1)} fusion(f32[1536,512,4]{1,0,2:T(8,128)S(1)} %get-tuple-element.623, f32[4,512]{1,0:T(4,128)S(1)} %get-tuple-element.624, pred[512,1536]{0,1:T(8,128)(4,1)S(1)} %compare_and_fusion.4), kind=kLoop, calls=%fused_computation.6.clone.1 | loop fusion | flops 12580864 | bytes 13385728 | tf_op jit(solution)/shard_map/while/body/eval_jaxpr/reduce_sum | solution.py:68
  98.6 8.2 %fusion.85 = bf16[128,4,512]{2,0,1:T(8,128)(2,1)S(1)} fusion(f32[1536,512,4]{1,0,2:T(8,128)} %copy-done.2, f32[4,512]{1,0:T(4,128)S(1)} %get-tuple-element.625, pred[512,1536]{0,1:T(8,128)(4,1)S(1)} %compare_and_fusion.4, bf16[2048,256]{1,0:T(8,128)(2,1)} %get-tuple-element.674, s32[]{:T(128)S(6)} %select_n.92, s32[]{:T(128)S(6)} %add.279), kind=kOutput, calls=%fused_computation.12.clone.1 | convolution fusion | flops 818151424 | bytes 14295048 | tf_op jit(solution)/shard_map/while/body/eval_jaxpr/kgqs,skd->qkgd/dot_general | solution.py:71
  107.9 1.3 copy.140
  109.2 1.6 broadcast_in_dim.82
  111.9 68.1 %while.33 = (s32[]{:T(128)}, f32[2048,256]{0,1:T(8,128)}, bf16[2,512,512]{2,1,0:T(8,128)(2,1)}, s32[2]{0:T(128)S(1)}, bf16[1024,512]{0,1:T(8,128)(2,1)}, /*index...) while((s32[]{:T(128)}, f32[2048,256]{0,1:T(8,128)}, ...), condition=%wide.region_10.11_spmd.clone, body=%wide.region_7.10_spmd.clone.sunk | while | flops 4063035392 | bytes 99607960 | solution.py:126
  114.2 7.4 %fusion.93 = f32[1536,512,4]{1,0,2:T(8,128)} fusion(bf16[512,4,128]{0,2,1:T(8,128)(2,1)S(1)} %bitcast.236, bf16[2048,256]{1,0:T(8,128)(2,1)} %get-tuple-element.728, s32[]{:T(128)S(6)} %select_n.95), kind=kOutput, calls=%fused_computation.56.clone.1 | convolution fusion | flops 805306368 | bytes 13500420 | tf_op jit(solution)/shard_map/while/body/eval_jaxpr/qkgd,skd->kgqs/dot_general | solution.py:58
  121.6 1.3 constant_dynamic-slice_fusion.8
  126.6 6.9 %fusion.95 = bf16[1,4,512,1536]{2,3,1,0:T(8,128)(2,1)S(1)} fusion(f32[1536,512,4]{1,0,2:T(8,128)} %fusion.93, bf16[512,4,128]{0,2,1:T(8,128)(2,1)S(1)} %bitcast.241, f32[4,512]{1,0:T(4,128)S(1)} %copy.189, f32[4,512]{1,0:T(4,128)S(1)} %dynamic-slice_bitcast_fusion.19, pred[512,1536]{0,1:T(8,128)(4,1)S(1)} %compare_and_fusion.5, ...), kind=kOutput, calls=%fused_computation.31.clone.1 | convolution fusion | flops 824180736 | bytes 20594696 | tf_op jit(solution)/shard_map/while/body/eval_jaxpr/qkgd,skd->kgqs/dot_general | solution.py:101
  133.5 2.1 fusion.96
  135.7 6.6 %fusion.94 = f32[1536,128]{0,1:T(8,128)S(1)} fusion(bf16[512,4,128]{0,2,1:T(8,128)(2,1)S(1)} %bitcast.242, f32[1536,512,4]{1,0,2:T(8,128)} %fusion.93, f32[4,512]{1,0:T(4,128)S(1)} %dynamic-slice_bitcast_fusion.19, pred[512,1536]{0,1:T(8,128)(4,1)} %copy-done.5), kind=kOutput, calls=%fused_computation.44.clone.1 | convolution fusion | flops 817889280 | bytes 14688256 | tf_op jit(solution)/shard_map/while/body/eval_jaxpr/kgqs,qkgd->skd/dot_general | solution.py:98
  142.6 2.3 fusion.98
  148.3 7.3 %fusion.93 = f32[1536,512,4]{1,0,2:T(8,128)} fusion(bf16[512,4,128]{0,2,1:T(8,128)(2,1)S(1)} %bitcast.236, bf16[2048,256]{1,0:T(8,128)(2,1)} %get-tuple-element.728, s32[]{:T(128)S(6)} %select_n.95), kind=kOutput, calls=%fused_computation.56.clone.1 | convolution fusion | flops 805306368 | bytes 13500420 | tf_op jit(solution)/shard_map/while/body/eval_jaxpr/qkgd,skd->kgqs/dot_general | solution.py:58
  160.6 6.9 %fusion.95 = bf16[1,4,512,1536]{2,3,1,0:T(8,128)(2,1)S(1)} fusion(f32[1536,512,4]{1,0,2:T(8,128)} %fusion.93, bf16[512,4,128]{0,2,1:T(8,128)(2,1)S(1)} %bitcast.241, f32[4,512]{1,0:T(4,128)S(1)} %copy.189, f32[4,512]{1,0:T(4,128)S(1)} %dynamic-slice_bitcast_fusion.19, pred[512,1536]{0,1:T(8,128)(4,1)S(1)} %compare_and_fusion.5, ...), kind=kOutput, calls=%fused_computation.31.clone.1 | convolution fusion | flops 824180736 | bytes 20594696 | tf_op jit(solution)/shard_map/while/body/eval_jaxpr/qkgd,skd->kgqs/dot_general | solution.py:101
  167.6 2.1 fusion.96
  169.7 6.6 %fusion.94 = f32[1536,128]{0,1:T(8,128)S(1)} fusion(bf16[512,4,128]{0,2,1:T(8,128)(2,1)S(1)} %bitcast.242, f32[1536,512,4]{1,0,2:T(8,128)} %fusion.93, f32[4,512]{1,0:T(4,128)S(1)} %dynamic-slice_bitcast_fusion.19, pred[512,1536]{0,1:T(8,128)(4,1)} %copy-done.5), kind=kOutput, calls=%fused_computation.44.clone.1 | convolution fusion | flops 817889280 | bytes 14688256 | tf_op jit(solution)/shard_map/while/body/eval_jaxpr/kgqs,qkgd->skd/dot_general | solution.py:98
  176.6 2.3 fusion.98
  180.0 1.3 slice.56
  181.4 1.9 collective-permute-start.1
  183.3 6.7 %collective-permute-done.1 = bf16[1024,256]{0,1:T(8,128)(2,1)S(1)} collective-permute-done((bf16[1024,256]{0,1:T(8,128)(2,1)S(1)}, bf16[1024,256]{0,1:T(8,128)(2,1)S(1)}, u32[]{:S(2)}, u32[]{:S(2)}) %collective-permute-start.1) | collective-permute-done | bytes 524320 | tf_op jit(solution)/shard_map/ppermute | solution.py:12
  190.0 1.4 add_convert_fusion
  192.2 7.5 %all-to-all-start.6 = ((bf16[8,128,128]{2,1,0:T(8,128)(2,1)}), bf16[8,128,128]{2,1,0:T(8,128)(2,1)S(1)}, u32[]{:S(2)}, u32[]{:S(2)}) async-start(bf16[8,128,128]{2,1,0:T(8,128)(2,1)} %bitcast.21), calls=%async_computation.6 | async-start | bytes 524288 | tf_op jit(solution)/shard_map/all_to_all | solution.py:135
  199.9 9.0 %all-to-all-done.6 = bf16[8,128,128]{2,1,0:T(8,128)(2,1)S(1)} async-done(((bf16[8,128,128]{2,1,0:T(8,128)(2,1)}), bf16[8,128,128]{2,1,0:T(8,128)(2,1)S(1)}, u32[]{:S(2)}, u32[]{:S(2)}) %all-to-all-start.6) | async-done | bytes 262176 | tf_op jit(solution)/shard_map/all_to_all | solution.py:135
  208.9 11.9 %all_to_all.152 = bf16[8,128,128]{2,1,0:T(8,128)(2,1)S(1)} all-to-all(bf16[8,128,128]{2,1,0:T(8,128)(2,1)S(1)} %bitcast.254), channel_id=1, replica_groups=mesh['blk'=32,'head'=8] {'head'}, dimensions={0} | all-to-all | bytes 524288 | tf_op jit(solution)/shard_map/all_to_all | solution.py:136
  220.9 20.1 %all_to_all.153 = bf16[8,128,512]{2,1,0:T(8,128)(2,1)S(1)} all-to-all(bf16[8,128,512]{2,1,0:T(8,128)(2,1)} %bitcast.246), channel_id=1, replica_groups=mesh['blk'=32,'head'=8] {'head'}, dimensions={0} | all-to-all | bytes 2097152 | tf_op jit(solution)/shard_map/all_to_all | solution.py:134
  241.0 3.6 %all-to-all-start.3 = ((bf16[8,128,512]{2,1,0:T(8,128)(2,1)}), bf16[8,128,512]{2,1,0:T(8,128)(2,1)S(1)}, u32[]{:S(2)}, u32[]{:S(2)}) async-start(bf16[8,128,512]{2,1,0:T(8,128)(2,1)} %bitcast.10), calls=%async_computation.3 | async-start | bytes 2097152 | tf_op jit(solution)/shard_map/all_to_all | solution.py:133
  247.3 1.3 copy.151
  248.6 10.3 %all-to-all-done.3 = bf16[8,128,512]{2,1,0:T(8,128)(2,1)S(1)} async-done(((bf16[8,128,512]{2,1,0:T(8,128)(2,1)}), bf16[8,128,512]{2,1,0:T(8,128)(2,1)S(1)}, u32[]{:S(2)}, u32[]{:S(2)}) %all-to-all-start.3) | async-done | bytes 1048608 | tf_op jit(solution)/shard_map/all_to_all | solution.py:133
  259.5 1.3 copy.150
  (102 shorter events, 33.9 us)
Async XLA Ops:
  0.6 1.0 copy-start
  2.3 15.6 %all-to-all-start = ((bf16[128,8,128]{2,0,1:T(8,128)(2,1)}), bf16[128,8,128]{2,0,1:T(8,128)(2,1)S(1)}, u32[]{:S(2)}, u32[]{:S(2)}) async-start(bf16[128,8,128]{2,0,1:T(8,128)(2,1)} %copy_bitcast_fusion.1), calls=%async_computation | async-start | bytes 524288 | tf_op jit(solution)/shard_map/all_to_all | solution.py:23
  18.0 11.8 %all-to-all-start.1 = ((bf16[128,8,128]{2,0,1:T(8,128)(2,1)}), bf16[128,8,128]{2,0,1:T(8,128)(2,1)S(1)}, u32[]{:S(2)}, u32[]{:S(2)}) async-start(bf16[128,8,128]{2,0,1:T(8,128)(2,1)} %copy_bitcast_fusion), calls=%async_computation.1 | async-start | bytes 524288 | tf_op jit(solution)/shard_map/all_to_all | solution.py:24
  29.8 20.3 %all-to-all-start.2 = ((bf16[128,8,512]{0,2,1:T(8,128)(2,1)}), bf16[128,8,512]{0,2,1:T(8,128)(2,1)S(1)}, u32[]{:S(2)}, u32[]{:S(2)}) async-start(bf16[128,8,512]{0,2,1:T(8,128)(2,1)} %bitcast.7), calls=%async_computation.2 | async-start | bytes 2097152 | tf_op jit(solution)/shard_map/all_to_all | solution.py:22
  33.4 15.6 %collective-permute-start = (bf16[1024,256]{1,0:T(8,128)(2,1)S(1)}, bf16[1024,256]{1,0:T(8,128)(2,1)S(1)}, u32[]{:S(2)}, u32[]{:S(2)}) collective-permute-start(bf16[1024,256]{1,0:T(8,128)(2,1)S(1)} %pad_maximum_fusion), channel_id=1, source_target_pairs={{0,8},{8,16},{16,24},{24,32},{32,40},{40,48},{48,56},{56,64},{64,7... | collective-permute-start | bytes 1572872 | tf_op jit(solution)/shard_map/ppermute | solution.py:12
  50.1 57.8 %all-to-all-start.4 = ((bf16[128,8,512]{0,2,1:T(8,128)(2,1)}), bf16[128,8,512]{0,2,1:T(8,128)(2,1)S(1)}, u32[]{:S(2)}, u32[]{:S(2)}) async-start(bf16[128,8,512]{0,2,1:T(8,128)(2,1)} %bitcast.14), calls=%async_computation.4 | async-start | bytes 2097152 | tf_op jit(solution)/shard_map/all_to_all | solution.py:25
  67.8 4.6 %copy-start.2 = (f32[1536,512,4]{1,0,2:T(8,128)}, f32[1536,512,4]{1,0,2:T(8,128)S(1)}, u32[]{:S(2)}) copy-start(f32[1536,512,4]{1,0,2:T(8,128)S(1)} %get-tuple-element.623) | copy-start | bytes 37748740 | tf_op jit(solution)/shard_map/while
  91.3 4.6 %copy-start.2 = (f32[1536,512,4]{1,0,2:T(8,128)}, f32[1536,512,4]{1,0,2:T(8,128)S(1)}, u32[]{:S(2)}) copy-start(f32[1536,512,4]{1,0,2:T(8,128)S(1)} %get-tuple-element.623) | copy-start | bytes 37748740 | tf_op jit(solution)/shard_map/while
  125.7 0.9 copy-start.5
  133.5 8.7 %copy-start.3 = (f32[2048,256]{0,1:T(8,128)S(1)}, f32[2048,256]{0,1:T(8,128)}, u32[]{:S(2)}) copy-start(f32[2048,256]{0,1:T(8,128)} %get-tuple-element.704) | copy-start | bytes 6291460 | tf_op jit(solution)/shard_map/while
  142.6 3.4 %copy-start.4 = (f32[2048,256]{0,1:T(8,128)}, f32[2048,256]{0,1:T(8,128)S(1)}, u32[]{:S(2)}) copy-start(f32[2048,256]{0,1:T(8,128)S(1)} %fusion.97) | copy-start | bytes 6291460 | tf_op jit(solution)/shard_map/while
  159.7 0.9 copy-start.5
  167.6 8.7 %copy-start.3 = (f32[2048,256]{0,1:T(8,128)S(1)}, f32[2048,256]{0,1:T(8,128)}, u32[]{:S(2)}) copy-start(f32[2048,256]{0,1:T(8,128)} %get-tuple-element.704) | copy-start | bytes 6291460 | tf_op jit(solution)/shard_map/while
  176.6 3.4 %copy-start.4 = (f32[2048,256]{0,1:T(8,128)}, f32[2048,256]{0,1:T(8,128)S(1)}, u32[]{:S(2)}) copy-start(f32[2048,256]{0,1:T(8,128)S(1)} %fusion.97) | copy-start | bytes 6291460 | tf_op jit(solution)/shard_map/while
  180.0 80.8 %copy-start.1 = (bf16[128,1024]{1,0:T(8,128)(2,1)S(1)}, bf16[128,1024]{1,0:T(8,128)(2,1)}, u32[]{:S(2)}) copy-start(bf16[128,1024]{1,0:T(8,128)(2,1)} %param.10) | copy-start | bytes 786436
  181.4 8.6 %collective-permute-start.1 = (bf16[1024,256]{0,1:T(8,128)(2,1)S(1)}, bf16[1024,256]{0,1:T(8,128)(2,1)S(1)}, u32[]{:S(2)}, u32[]{:S(2)}) collective-permute-start(bf16[1024,256]{0,1:T(8,128)(2,1)S(1)} %slice.56), channel_id=1, source_target_pairs={{8,0},{16,8},{24,16},{32,24},{40,32},{48,40},{56,48},{64,56},{72,6... | collective-permute-start | bytes 1572872 | tf_op jit(solution)/shard_map/ppermute | solution.py:12
  192.2 16.7 %all-to-all-start.6 = ((bf16[8,128,128]{2,1,0:T(8,128)(2,1)}), bf16[8,128,128]{2,1,0:T(8,128)(2,1)S(1)}, u32[]{:S(2)}, u32[]{:S(2)}) async-start(bf16[8,128,128]{2,1,0:T(8,128)(2,1)} %bitcast.21), calls=%async_computation.6 | async-start | bytes 524288 | tf_op jit(solution)/shard_map/all_to_all | solution.py:135
  241.0 17.9 %all-to-all-start.3 = ((bf16[8,128,512]{2,1,0:T(8,128)(2,1)}), bf16[8,128,512]{2,1,0:T(8,128)(2,1)S(1)}, u32[]{:S(2)}, u32[]{:S(2)}) async-start(bf16[8,128,512]{2,1,0:T(8,128)(2,1)} %bitcast.10), calls=%async_computation.3 | async-start | bytes 2097152 | tf_op jit(solution)/shard_map/all_to_all | solution.py:133
where the time goes:
time: 264 us; the launch traced here: 261 us
  matrix products  73.4 us (28%)
  local copies, waits for them, and re-layouts  51.5 us (20%)
  waiting for transfers between devices  48.9 us (19%)
  starting transfers between devices  35 us (13%)
  blocking collectives  32 us (12%)
  other arithmetic  16.3 us (6%)
  loops' own time  3 us (1%)
    dot_general x4, matrix products, tile_scores(): jnp.einsum('qkgd,skd->kgqs', query_rows, key_rows, preferred_element_type...  21 us
    all_to_all x1, blocking collectives, per_device(): lax.all_to_all(grad_query_heads, 'head', split_axis=0, concat_axis=1, til...  20.1 us
    dot_general x2, matrix products, forward_tile(): jnp.einsum('kgqs,skd->qkgd', weights_bf, value_rows, preferred_element_ty...  16.5 us
    ppermute x2, waiting for transfers between devices, passed_along(): lax.ppermute(value, axis, [(source, source + steps) for source in range(i...  16.4 us
    dot_general x2, matrix products, backward_tile(): jnp.einsum('qkgd,skd->kgqs', grad_rows, value_rows, preferred_element_typ...  13.8 us
    dot_general x2, matrix products, backward_tile(): jnp.einsum('kgqs,qkgd->skd', weights_bf, grad_rows, preferred_element_typ...  13.1 us
    unnamed x11, local copies, waits for them, and re-layouts  12.1 us
    all_to_all x1, blocking collectives, per_device(): lax.all_to_all(grad_value_heads, 'head', split_axis=0, concat_axis=1, til...  11.9 us
  transfers between devices with their start and end apart: 8, of which 6 were waited for; matrix products, arithmetic and copies ran while one was open for 21% of the time, Pallas kernels for 0%

commit v1 on v0

v1 whole, which is shorter than its diff:
```python
import functools
import math

import jax
import jax.numpy as jnp
from jax import lax
from jax.experimental import pallas as pl
from jax.experimental.pallas import tpu as pltpu
from jax.sharding import PartitionSpec as P

HEAD_DIM = 128
SCALE = HEAD_DIM**-0.5
SCALE_LOG2 = SCALE * math.log2(math.e)
FLOOR = -1e30
TILE_Q = 256
TILE_K = 256
LAST_DIMS = (((1,), (1,)), ((), ()))


def passed_along(value, axis, steps):
    count = lax.axis_size(axis)
    initial, last = (max(0, -steps), min(count, count - steps))
    return lax.ppermute(value, axis, [(source, source + steps) for source in range(initial, last)])


def attention_kernel(heads, block, first, last, lo_ref, start_ref, rows_ref, earlier_ref, own_ref, *refs):
    if first:
        carried_ref = None
    else:
        carried_ref, refs = refs[0], refs[1:]
    out_ref, refs = refs[0], refs[1:]
    if last:
        earlier_out, own_out, refs = refs[0], refs[1], refs[2:]
    else:
        sums_out, refs = refs[0], refs[1:]
    window, scores, sums, peaks, totals, attended, grad_query = refs
    tile, tiles = pl.program_id(0), pl.num_programs(0)
    stacked = heads * TILE_Q

    @pl.when(tile == 0)
    def _():
        window[:block] = earlier_ref[...]
        window[block:] = own_ref[...]
        sums[...] = jnp.zeros_like(sums) if first else carried_ref[...]

    lo = lo_ref[tile]
    hi = (block + (tile + 1) * TILE_Q - 1) // TILE_K + 1

    def stack(base):
        return jnp.concatenate(
            [rows_ref[:, base + h * HEAD_DIM : base + (h + 1) * HEAD_DIM] for h in range(heads)], axis=0
        )

    query = stack(0)
    grad = stack(heads * HEAD_DIM)
    row = block + tile * TILE_Q + lax.broadcasted_iota(jnp.int32, (TILE_Q, TILE_K), 0)
    start = start_ref[...]
    peaks[...] = jnp.full_like(peaks, FLOOR)
    totals[...] = jnp.zeros_like(totals)
    attended[...] = jnp.zeros_like(attended)
    grad_query[...] = jnp.zeros_like(grad_query)

    @pl.loop(lo, hi)
    def _(step):
        base = pl.multiple_of(step * TILE_K, TILE_K)
        product = lax.dot_general(
            query, window[pl.ds(base, TILE_K), :HEAD_DIM], LAST_DIMS, preferred_element_type=jnp.float32
        )
        column = base + lax.broadcasted_iota(jnp.int32, (TILE_Q, TILE_K), 1)
        kept = (column <= row) & (column >= start)
        product = jnp.where(kept[None], product.reshape(heads, TILE_Q, TILE_K) * SCALE_LOG2, FLOOR)
        product = product.reshape(stacked, TILE_K)
        scores[step - lo] = product
        peak = peaks[...]
        for j in range(TILE_K // 128):
            peak = jnp.maximum(peak, product[:, j * 128 : (j + 1) * 128])
        peaks[...] = peak

    peak = jnp.max(peaks[...], axis=1, keepdims=True)

    @pl.loop(lo, hi)
    def _(step):
        base = pl.multiple_of(step * TILE_K, TILE_K)
        weights = jnp.exp2(scores[step - lo] - peak)
        scores[step - lo] = weights
        total = totals[...]
        for j in range(TILE_K // 128):
            total = total + weights[:, j * 128 : (j + 1) * 128]
        totals[...] = total
        attended[...] += jnp.dot(
            weights.astype(jnp.bfloat16), window[pl.ds(base, TILE_K), HEAD_DIM:], preferred_element_type=jnp.float32
        )

    inverse = 1.0 / jnp.sum(totals[...], axis=1, keepdims=True)
    out = (attended[...] * inverse).astype(jnp.bfloat16)
    grad_wide = grad.astype(jnp.float32)
    delta = jnp.sum(grad_wide * out.astype(jnp.float32), axis=1, keepdims=True)
    grad_across = (grad_wide * inverse).astype(jnp.bfloat16).T
    query_across = (query.astype(jnp.float32) * (inverse * SCALE)).astype(jnp.bfloat16).T

    @pl.loop(lo, hi)
    def _(step):
        base = pl.multiple_of(step * TILE_K, TILE_K)
        span = pl.ds(base, TILE_K)
        keys = window[span, :HEAD_DIM]
        weights = scores[step - lo]
        grad_weights = lax.dot_general(grad, window[span, HEAD_DIM:], LAST_DIMS, preferred_element_type=jnp.float32)
        grad_scores = (weights * (grad_weights - delta)).astype(jnp.bfloat16)
        grad_query[...] += jnp.dot(grad_scores, keys, preferred_element_type=jnp.float32)
        sums[:HEAD_DIM, span] += jnp.dot(query_across, grad_scores, preferred_element_type=jnp.float32)
        sums[HEAD_DIM:, span] += jnp.dot(
            grad_across, weights.astype(jnp.bfloat16), preferred_element_type=jnp.float32
        )

    grad_rows = (grad_query[...] * (inverse * SCALE)).astype(jnp.bfloat16)
    for h in range(heads):
        out_ref[:, h * HEAD_DIM : (h + 1) * HEAD_DIM] = out[h * TILE_Q : (h + 1) * TILE_Q]
        out_ref[:, (heads + h) * HEAD_DIM : (heads + h + 1) * HEAD_DIM] = grad_rows[h * TILE_Q : (h + 1) * TILE_Q]

    @pl.when(tile == tiles - 1)
    def _():
        if last:
            earlier_out[...] = sums[:, :block].astype(jnp.bfloat16).T
            own_out[...] = sums[:, block:].T
        else:
            sums_out[...] = sums[...]


def attention(rows, earlier, own, carried, start, lo, last):
    block, width = rows.shape
    heads = width // (2 * HEAD_DIM)
    pair = own.shape[1]
    stacked = heads * TILE_Q
    most = block // TILE_K + 1
    first = carried is None
    whole = lambda t, _: (0, 0)
    by_tile = lambda t, _: (t, 0)
    in_specs = [
        pl.BlockSpec((TILE_Q, 1), by_tile),
        pl.BlockSpec((TILE_Q, width), by_tile),
        pl.BlockSpec((block, pair), whole),
        pl.BlockSpec((block, pair), whole),
    ]
    operands = [start, rows, earlier, own]
    if not first:
        in_specs.append(pl.BlockSpec((pair, 2 * block), whole))
        operands.append(carried)
    out_specs = [pl.BlockSpec((TILE_Q, width), by_tile)]
    out_shape = [jax.ShapeDtypeStruct((block, width), jnp.bfloat16)]
    if last:
        out_specs += [pl.BlockSpec((block, pair), whole)] * 2
        out_shape += [
            jax.ShapeDtypeStruct((block, pair), jnp.bfloat16),
            jax.ShapeDtypeStruct((block, pair), jnp.float32),
        ]
    else:
        out_specs.append(pl.BlockSpec((pair, 2 * block), whole))
        out_shape.append(jax.ShapeDtypeStruct((pair, 2 * block), jnp.float32))
    pairs = heads * block * block
    return pl.pallas_call(
        functools.partial(attention_kernel, heads, block, first, last),
        grid_spec=pltpu.PrefetchScalarGridSpec(
            num_scalar_prefetch=1,
            grid=(block // TILE_Q,),
            in_specs=in_specs,
            out_specs=out_specs,
            scratch_shapes=[
                pltpu.VMEM((2 * block, pair), jnp.bfloat16),
                pltpu.VMEM((most, stacked, TILE_K), jnp.float32),
                pltpu.VMEM((pair, 2 * block), jnp.float32),
                pltpu.VMEM((stacked, 128), jnp.float32),
                pltpu.VMEM((stacked, 128), jnp.float32),
                pltpu.VMEM((stacked, HEAD_DIM), jnp.float32),
                pltpu.VMEM((stacked, HEAD_DIM), jnp.float32),
            ],
        ),
        out_shape=out_shape,
        compiler_params=pltpu.CompilerParams(vmem_limit_bytes=40 << 20),
        cost_estimate=pl.CostEstimate(
            flops=12 * pairs * HEAD_DIM, bytes_accessed=4 * block * width, transcendentals=pairs
        ),
        name="attention_" + ("first" if first else "last"),
    )(lo, *operands)


def exchange(value):
    return lax.all_to_all(value, "head", split_axis=0, concat_axis=0, tiled=True)


def per_device(query, key, value, grad_out, doc_lengths):
    rows = query.shape[0]
    count = lax.axis_size("head")
    block = rows * count
    pair = 2 * HEAD_DIM
    groups = query.shape[1] // key.shape[1]
    half = groups // 2
    by_head = lambda x: x.reshape(rows, count, -1)

    doc_ends = jnp.cumsum(doc_lengths)
    doc_starts = doc_ends - doc_lengths
    origin = lax.axis_index("blk") * block - block
    positions = origin + block + jnp.arange(block, dtype=jnp.int32)
    starts = jnp.max(jnp.where(doc_starts[None, :] <= positions[:, None], doc_starts[None, :], 0), axis=1)
    starts = starts - origin
    lo = jnp.maximum(starts[::TILE_Q] // TILE_K, 0).astype(jnp.int32)
    starts = starts.astype(jnp.int32)[:, None]

    key_value = jnp.concatenate([by_head(key), by_head(value)], axis=2).transpose(1, 0, 2)
    own = exchange(key_value).reshape(block, pair)
    earlier = passed_along(own, "blk", 1)

    def entering(g):
        span = slice(g * half * HEAD_DIM, (g + 1) * half * HEAD_DIM)
        packed = jnp.concatenate([by_head(query)[:, :, span], by_head(grad_out)[:, :, span]], axis=2)
        return exchange(packed.transpose(1, 0, 2)).reshape(block, groups * HEAD_DIM)

    rows_first = entering(0)
    rows_last = entering(1)
    out_first, carried = attention(rows_first, earlier, own, None, starts, lo, False)
    back_first = exchange(out_first.reshape(count, rows, -1))
    out_last, earlier_sums, own_sums = attention(rows_last, earlier, own, carried, starts, lo, True)
    back_last = exchange(out_last.reshape(count, rows, -1))
    returned = passed_along(earlier_sums, "blk", -1)
    pair_sums = (own_sums + returned.astype(jnp.float32)).astype(jnp.bfloat16)
    back_pair = exchange(pair_sums.reshape(count, rows, pair))

    middle = half * HEAD_DIM
    attended = jnp.concatenate([back_first[:, :, :middle], back_last[:, :, :middle]], axis=2)
    grad_query = jnp.concatenate([back_first[:, :, middle:], back_last[:, :, middle:]], axis=2)
    flat = lambda x: x.transpose(1, 0, 2).reshape(rows, -1)
    return (
        flat(attended),
        flat(grad_query),
        flat(back_pair[:, :, :HEAD_DIM]),
        flat(back_pair[:, :, HEAD_DIM:]),
    )


def solution(mesh):
    spec = P(("blk", "head"), None)
    return jax.shard_map(
        per_device,
        mesh=mesh,
        in_specs=(spec, spec, spec, spec, P()),
        out_specs=(spec, spec, spec, spec),
        check_vma=False,
    )
```

time: 264 us -> 167 us (0.63); the launches traced: 261 us -> 167 us
  matrix products: 73.4 us -> 0 us
  Pallas kernels: 0 us -> 37.8 us
  local copies, waits for them, and re-layouts: 51.5 us -> 13.7 us
  blocking collectives: 32 us -> 0 us
  waiting for transfers between devices: 48.9 us -> 75.1 us
  other arithmetic: 16.3 us -> 4.4 us
  loops' own time: 3 us -> 0 us
    dot_general x14 -> x0, matrix products: 73.4 us -> none  [the longest x4 21 us: tile_scores(): jnp.einsum('qkgd,skd->kgqs', query_rows, key_rows, preferred_element_type...]
    pallas_call x0 -> x2, Pallas kernels: none -> 37.8 us  [attention(): pl.pallas_call(functools.partial(attention_kernel, heads, block, first, l...]
    all_to_all x2 -> x0, blocking collectives: 32 us -> none  [the longest x1 20.1 us: per_device(): lax.all_to_all(grad_query_heads, 'head', split_axis=0, concat_axis=1, til...]
    all_to_all x6, waiting for transfers between devices: 32.4 us -> 61.6 us  [exchange(): lax.all_to_all(value, 'head', split_axis=0, concat_axis=0, tiled=True)]
    while x18 -> x0, local copies, waits for them, and re-layouts: 11.5 us -> none
    dynamic_slice x12 -> x0, local copies, waits for them, and re-layouts: 9.62 us -> none  [the longest x4 4.33 us: tile_scores(): lax.dynamic_slice_in_dim(query_heads, first_row, tile_rows, 0)]
    all_to_all x8 -> x0, local copies, waits for them, and re-layouts: 6.73 us -> none  [the longest x1 1.7 us: per_device(): lax.all_to_all(value, 'head', split_axis=1, concat_axis=0, tiled=True)]
    reduce_sum x10 -> x0, other arithmetic: 6.29 us -> none  [the longest x2 5.42 us: forward_tile(): jnp.sum(jnp.exp(scores - peak_score), axis=-1, keepdims=True)]
  transfers between devices with their start and end apart: 8 -> 8, of which waited for: 6 -> 6; matrix products, arithmetic and copies ran while one was open for 21% -> 5% of each run, Pallas kernels for 0% -> 11%
where the time goes in v1:
time: 167 us
  waiting for transfers between devices  75.1 us (45%)
  Pallas kernels  37.8 us (23%)
  starting transfers between devices  35.2 us (21%)
  local copies, waits for them, and re-layouts  13.7 us (8%)
  other arithmetic  4.4 us (3%)
    all_to_all x6, waiting for transfers between devices, exchange(): lax.all_to_all(value, 'head', split_axis=0, concat_axis=0, tiled=True)  61.6 us
    pallas_call x2, Pallas kernels, attention(): pl.pallas_call(functools.partial(attention_kernel, heads, block, first, l...  37.8 us
    all_to_all x6, starting transfers between devices, exchange(): lax.all_to_all(value, 'head', split_axis=0, concat_axis=0, tiled=True)  31.3 us
    ppermute x2, waiting for transfers between devices, passed_along(): lax.ppermute(value, axis, [(source, source + steps) for source in range(i...  13.5 us
    unnamed x23, local copies, waits for them, and re-layouts  7.04 us
    ppermute x2, starting transfers between devices, passed_along(): lax.ppermute(value, axis, [(source, source + steps) for source in range(i...  3.84 us
    reshape x4, local copies, waits for them, and re-layouts, per_device(): flat = lambda x: x.transpose(1, 0, 2).reshape(rows, -1)  3.69 us
  transfers between devices with their start and end apart: 8, of which 6 were waited for; matrix products, arithmetic and copies ran while one was open for 5% of the time, Pallas kernels for 11%

profile of v1, /device:TPU:192, one launch (start us, length us, event | category | flops | bytes accessed | tf_op | source)
XLA Modules:
  0.0 167.0 jit_solution(4007857467895516948)
XLA Ops:
  0.7 0.9 copy-done
  1.6 1.1 copy_bitcast_fusion.2
  2.7 0.9 maximum_bitcast_fusion.4
  3.5 6.9 %all-to-all-start.1 = ((bf16[8,128,256]{2,1,0:T(8,128)(2,1)}), bf16[8,128,256]{2,1,0:T(8,128)(2,1)S(1)}, u32[]{:S(2)}, u32[]{:S(2)}) async-start(bf16[8,128,256]{2,1,0:T(8,128)(2,1)} %maximum_bitcast_fusion.4), calls=%async_computation.1 | async-start | bytes 1048576 | tf_op jit(solution)/shard_map/all_to_all | solution.py:187
  10.5 0.4 copy.56
  10.9 0.1 fusion.3
  11.0 0.1 copy.46
  11.1 1.0 copy-done.6
  12.1 0.4 copy.57
  12.6 0.1 copy.47
  12.7 1.1 maximum_bitcast_fusion
  13.7 7.6 %all-to-all-done.1 = bf16[8,128,256]{2,1,0:T(8,128)(2,1)S(1)} async-done(((bf16[8,128,256]{2,1,0:T(8,128)(2,1)}), bf16[8,128,256]{2,1,0:T(8,128)(2,1)S(1)}, u32[]{:S(2)}, u32[]{:S(2)}) %all-to-all-start.1) | async-done | bytes 524320 | tf_op jit(solution)/shard_map/all_to_all | solution.py:187
  21.3 3.6 %all-to-all-start = ((bf16[8,128,512]{2,1,0:T(8,128)(2,1)}), bf16[8,128,512]{2,1,0:T(8,128)(2,1)S(1)}, u32[]{:S(2)}, u32[]{:S(2)}) async-start(bf16[8,128,512]{2,1,0:T(8,128)(2,1)} %maximum_bitcast_fusion), calls=%async_computation | async-start | bytes 2097152 | tf_op jit(solution)/shard_map/all_to_all | solution.py:187
  24.9 0.1 copy.48
  25.0 0.1 copy.49
  25.1 1.1 maximum_bitcast_fusion.1
  26.2 13.9 %all-to-all-done = bf16[8,128,512]{2,1,0:T(8,128)(2,1)S(1)} async-done(((bf16[8,128,512]{2,1,0:T(8,128)(2,1)}), bf16[8,128,512]{2,1,0:T(8,128)(2,1)S(1)}, u32[]{:S(2)}, u32[]{:S(2)}) %all-to-all-start) | async-done | bytes 1048608 | tf_op jit(solution)/shard_map/all_to_all | solution.py:187
  40.2 4.2 %all-to-all-start.3 = ((bf16[8,128,512]{2,1,0:T(8,128)(2,1)}), bf16[8,128,512]{2,1,0:T(8,128)(2,1)S(1)}, u32[]{:S(2)}, u32[]{:S(2)}) async-start(bf16[8,128,512]{2,1,0:T(8,128)(2,1)} %maximum_bitcast_fusion.1), calls=%async_computation.3 | async-start | bytes 2097152 | tf_op jit(solution)/shard_map/all_to_all | solution.py:187
  44.4 0.1 copy.33
  44.5 0.1 reduce-window.9
  44.5 0.1 reduce
  44.7 1.9 %collective-permute-start = (bf16[1024,256]{1,0:T(8,128)(2,1)S(1)}, bf16[1024,256]{1,0:T(8,128)(2,1)}, u32[]{:S(2)}, u32[]{:S(2)}) collective-permute-start(bf16[1024,256]{1,0:T(8,128)(2,1)S(1)} %bitcast.50), channel_id=1, source_target_pairs={{0,8},{8,16},{16,24},{24,32},{32,40},{40,48},{48,56},{56,64},{64,7... | collective-permute-start | bytes 1572872 | tf_op jit(solution)/shard_map/ppermute | solution.py:23
  46.6 0.1 select_reduce_fusion
  46.7 0.1 slice.33
  46.8 0.2 copy.38.start_ref
  47.1 13.5 %collective-permute-done.earlier_ref = bf16[1024,256]{1,0:T(8,128)(2,1)} collective-permute-done((bf16[1024,256]{1,0:T(8,128)(2,1)S(1)}, bf16[1024,256]{1,0:T(8,128)(2,1)}, u32[]{:S(2)}, u32[]{:S(2)}) %collective-permute-start) | collective-permute-done | bytes 524320 | tf_op jit(solution)/shard_map/ppermute | solution.py:23
  60.6 18.7 %attention_first.1 = (bf16[1024,512]{1,0:T(8,128)(2,1)}, f32[256,2048]{1,0:T(8,128)S(1)}) custom-call(s32[4]{0:T(128)S(1)} %fusion.lo_ref, s32[1024,1]{1,0:T(8,128)S(1)} %copy.38.start_ref, bf16[1024,512]{1,0:T(8,128)(2,1)S(1)} %bitcast.48, bf16[1024,256]{1,0:T(8,128)(2,1)} %collective-permute-done.earlier_ref, bf16[1024,256]{1,0:T(8,128)(2,1)S(1)} %bitcast.51), custom_call_target="tpu_custom_call" | custom-call | flops 3221225472 | bytes 2097152 | tf_op jit(solution)/shard_map/attention_first/pallas_call | solution.py:160
  79.3 1.3 copy-done.3
  80.6 1.6 copy-done.4
  82.2 19.0 %attention_last.1 = (bf16[1024,512]{1,0:T(8,128)(2,1)}, bf16[1024,256]{1,0:T(8,128)(2,1)S(1)}, f32[1024,256]{1,0:T(8,128)S(1)}) custom-call(s32[4]{0:T(128)S(1)} %fusion.lo_ref, s32[1024,1]{1,0:T(8,128)S(1)} %copy.38.start_ref, bf16[1024,512]{1,0:T(8,128)(2,1)S(1)} %bitcast.49, bf16[1024,256]{1,0:T(8,128)(2,1)} %collective-permute-done.earlier_ref, ...), custom_call_target="tpu_custom_call" | custom-call | flops 3221225472 | bytes 2097152 | tf_op jit(solution)/shard_map/attention_last/pallas_call | solution.py:160
  101.3 0.8 copy-done.1
  102.1 8.2 %all-to-all-start.4 = ((bf16[8,128,512]{2,1,0:T(8,128)(2,1)}), bf16[8,128,512]{2,1,0:T(8,128)(2,1)S(1)}, u32[]{:S(2)}, u32[]{:S(2)}) async-start(bf16[8,128,512]{2,1,0:T(8,128)(2,1)} %bitcast.9), calls=%async_computation.4 | async-start | bytes 2097152 | tf_op jit(solution)/shard_map/all_to_all | solution.py:187
  110.3 1.9 %collective-permute-start.1 = (bf16[1024,256]{1,0:T(8,128)(2,1)S(1)}, bf16[1024,256]{1,0:T(8,128)(2,1)S(1)}, u32[]{:S(2)}, u32[]{:S(2)}) collective-permute-start(bf16[1024,256]{1,0:T(8,128)(2,1)S(1)} %copy-done.2), channel_id=1, source_target_pairs={{8,0},{16,8},{24,16},{32,24},{40,32},{48,40},{56,48},{64,56},{72,6... | collective-permute-start | bytes 1572872 | tf_op jit(solution)/shard_map/ppermute | solution.py:23
  112.3 18.8 %all-to-all-done.4 = bf16[8,128,512]{2,1,0:T(8,128)(2,1)S(1)} async-done(((bf16[8,128,512]{2,1,0:T(8,128)(2,1)}), bf16[8,128,512]{2,1,0:T(8,128)(2,1)S(1)}, u32[]{:S(2)}, u32[]{:S(2)}) %all-to-all-start.4) | async-done | bytes 1048608 | tf_op jit(solution)/shard_map/all_to_all | solution.py:187
  131.0 4.2 %all-to-all-start.2 = ((bf16[8,128,512]{2,1,0:T(8,128)(2,1)}), bf16[8,128,512]{2,1,0:T(8,128)(2,1)}, u32[]{:S(2)}, u32[]{:S(2)}) async-start(bf16[8,128,512]{2,1,0:T(8,128)(2,1)} %bitcast.6), calls=%async_computation.2 | async-start | bytes 2097152 | tf_op jit(solution)/shard_map/all_to_all | solution.py:187
  135.3 0.9 add_convert_fusion
  136.2 0.1 fusion.2
  136.3 14.4 %all-to-all-done.2 = bf16[8,128,512]{2,1,0:T(8,128)(2,1)} async-done(((bf16[8,128,512]{2,1,0:T(8,128)(2,1)}), bf16[8,128,512]{2,1,0:T(8,128)(2,1)}, u32[]{:S(2)}, u32[]{:S(2)}) %all-to-all-start.2) | async-done | bytes 1048608 | tf_op jit(solution)/shard_map/all_to_all | solution.py:187
  150.8 4.2 %all-to-all-start.5 = ((bf16[8,128,256]{2,1,0:T(8,128)(2,1)}), bf16[8,128,256]{2,1,0:T(8,128)(2,1)S(1)}, u32[]{:S(2)}, u32[]{:S(2)}) async-start(bf16[8,128,256]{2,1,0:T(8,128)(2,1)} %bitcast.12), calls=%async_computation.5 | async-start | bytes 1048576 | tf_op jit(solution)/shard_map/all_to_all | solution.py:187
  154.9 1.3 fusion.1
  156.2 0.1 maximum_bitcast_fusion.3
  156.3 1.1 copy.53
  157.4 0.1 maximum_bitcast_fusion.2
  157.5 1.1 copy.52
  158.6 6.8 %all-to-all-done.5 = bf16[8,128,256]{2,1,0:T(8,128)(2,1)S(1)} async-done(((bf16[8,128,256]{2,1,0:T(8,128)(2,1)}), bf16[8,128,256]{2,1,0:T(8,128)(2,1)S(1)}, u32[]{:S(2)}, u32[]{:S(2)}) %all-to-all-start.5) | async-done | bytes 524320 | tf_op jit(solution)/shard_map/all_to_all | solution.py:187
  165.4 0.1 slice_bitcast_fusion
  165.5 0.8 copy.62
  166.3 0.8 copy.63
  (18 shorter events, 0.1 us)
Async XLA Ops:
  0.6 1.0 copy-start
  0.6 9.8 %copy-start.5 = (bf16[128,4096]{1,0:T(8,128)(2,1)S(1)}, bf16[128,4096]{1,0:T(8,128)(2,1)}, u32[]{:S(2)}) copy-start(bf16[128,4096]{1,0:T(8,128)(2,1)} %param.5) | copy-start | bytes 3145732
  3.5 17.8 %all-to-all-start.1 = ((bf16[8,128,256]{2,1,0:T(8,128)(2,1)}), bf16[8,128,256]{2,1,0:T(8,128)(2,1)S(1)}, u32[]{:S(2)}, u32[]{:S(2)}) async-start(bf16[8,128,256]{2,1,0:T(8,128)(2,1)} %maximum_bitcast_fusion.4), calls=%async_computation.1 | async-start | bytes 1048576 | tf_op jit(solution)/shard_map/all_to_all | solution.py:187
  10.9 1.2 copy-start.6
  21.3 18.8 %all-to-all-start = ((bf16[8,128,512]{2,1,0:T(8,128)(2,1)}), bf16[8,128,512]{2,1,0:T(8,128)(2,1)S(1)}, u32[]{:S(2)}, u32[]{:S(2)}) async-start(bf16[8,128,512]{2,1,0:T(8,128)(2,1)} %maximum_bitcast_fusion), calls=%async_computation | async-start | bytes 2097152 | tf_op jit(solution)/shard_map/all_to_all | solution.py:187
  25.1 19.2 %copy-start.7 = (s32[64]{0:T(128)S(1)}, s32[64]{0:T(128)}, u32[]{:S(2)}) copy-start(s32[64]{0:T(128)} %param.9) | copy-start | bytes 772
  40.2 40.5 %all-to-all-start.3 = ((bf16[8,128,512]{2,1,0:T(8,128)(2,1)}), bf16[8,128,512]{2,1,0:T(8,128)(2,1)S(1)}, u32[]{:S(2)}, u32[]{:S(2)}) async-start(bf16[8,128,512]{2,1,0:T(8,128)(2,1)} %maximum_bitcast_fusion.1), calls=%async_computation.3 | async-start | bytes 2097152 | tf_op jit(solution)/shard_map/all_to_all | solution.py:187
  44.7 15.9 %collective-permute-start = (bf16[1024,256]{1,0:T(8,128)(2,1)S(1)}, bf16[1024,256]{1,0:T(8,128)(2,1)}, u32[]{:S(2)}, u32[]{:S(2)}) collective-permute-start(bf16[1024,256]{1,0:T(8,128)(2,1)S(1)} %bitcast.50), channel_id=1, source_target_pairs={{0,8},{8,16},{16,24},{24,32},{32,40},{40,48},{48,56},{56,64},{64,7... | collective-permute-start | bytes 1572872 | tf_op jit(solution)/shard_map/ppermute | solution.py:23
  79.3 1.3 copy-start.3
  80.6 1.6 copy-start.4
  101.3 0.8 copy-start.1
  102.1 8.2 %copy-start.2 = (bf16[1024,256]{1,0:T(8,128)(2,1)S(1)}, bf16[1024,256]{1,0:T(8,128)(2,1)}, u32[]{:S(2)}) copy-start(bf16[1024,256]{1,0:T(8,128)(2,1)} %copy-done.1) | copy-start | bytes 1572868
  102.1 29.0 %all-to-all-start.4 = ((bf16[8,128,512]{2,1,0:T(8,128)(2,1)}), bf16[8,128,512]{2,1,0:T(8,128)(2,1)S(1)}, u32[]{:S(2)}, u32[]{:S(2)}) async-start(bf16[8,128,512]{2,1,0:T(8,128)(2,1)} %bitcast.9), calls=%async_computation.4 | async-start | bytes 2097152 | tf_op jit(solution)/shard_map/all_to_all | solution.py:187
  110.3 25.0 %collective-permute-start.1 = (bf16[1024,256]{1,0:T(8,128)(2,1)S(1)}, bf16[1024,256]{1,0:T(8,128)(2,1)S(1)}, u32[]{:S(2)}, u32[]{:S(2)}) collective-permute-start(bf16[1024,256]{1,0:T(8,128)(2,1)S(1)} %copy-done.2), channel_id=1, source_target_pairs={{8,0},{16,8},{24,16},{32,24},{40,32},{48,40},{56,48},{64,56},{72,6... | collective-permute-start | bytes 1572872 | tf_op jit(solution)/shard_map/ppermute | solution.py:23
  131.0 19.7 %all-to-all-start.2 = ((bf16[8,128,512]{2,1,0:T(8,128)(2,1)}), bf16[8,128,512]{2,1,0:T(8,128)(2,1)}, u32[]{:S(2)}, u32[]{:S(2)}) async-start(bf16[8,128,512]{2,1,0:T(8,128)(2,1)} %bitcast.6), calls=%async_computation.2 | async-start | bytes 2097152 | tf_op jit(solution)/shard_map/all_to_all | solution.py:187
  150.8 14.6 %all-to-all-start.5 = ((bf16[8,128,256]{2,1,0:T(8,128)(2,1)}), bf16[8,128,256]{2,1,0:T(8,128)(2,1)S(1)}, u32[]{:S(2)}, u32[]{:S(2)}) async-start(bf16[8,128,256]{2,1,0:T(8,128)(2,1)} %bitcast.12), calls=%async_computation.5 | async-start | bytes 1048576 | tf_op jit(solution)/shard_map/all_to_all | solution.py:187
